TPU v7x, 128 devices: a whole 4x4x4 slice. The times are simulated.
128 devices in a mesh: rows: 32 (over x, z, core), rel: 4 (over y).
Axes of the slice: x: 4, y: 4, z: 4, core: 2. Of those that a mesh axis runs over, the one named last changes fastest.
Arguments:
- features: bfloat16 [16384, 256], P('rows'), may hold values from -6 to 6
- bases: bfloat16 [8, 256, 256], replicated, may hold values from -0.125 to 0.125
- root: bfloat16 [256, 256], replicated, may hold values from -0.375 to 0.375
- coeffs: float32 [800, 8], P('rel'), may hold values from -4 to 4
- tiles: bfloat16 [32, 4, 64, 128, 128], P('rows', 'rel'), as said below
- tile_dst: int32 [32, 4, 64], P('rows', 'rel'), may hold values from 0 to 3
- tile_src: int32 [32, 4, 64], P('rows', 'rel'), may hold values from 0 to 63
- tile_rel: int32 [32, 4, 64], P('rows', 'rel'), may hold values from 0 to 199
- tile_live: int32 [32, 4], P('rows', 'rel'), may hold values from 16 to 64, as said below
- send_list: int32 [32, 4, 32, 2], P('rows', 'rel'), may hold values from 0 to 3
- cotangent: bfloat16 [16384, 256], P('rows'), may hold values from -6 to 6
Outputs:
- output: bfloat16 [16384, 256], P('rows')
- feature_grad: float32 [16384, 256], P('rows')
- basis_grad: float32 [8, 256, 256], replicated
- root_grad: float32 [256, 256], replicated
Inputs may be any that keep to these rules, and one draw needn't show every extreme that they name: `tile_live`: at least one device uses all 64 tile slots. `tiles`: entries are zero or positive, at most 12 / sqrt(2048).
All inputs are finite; a program needn't handle non-finite values.
Results may differ from a plain program's by a relative error of at most 0.0029.
Values may be sent and summed in bfloat16 or wider, within the bound.
A program may use at most 128 MiB of HBM per device.

v0:
```python
import math
import jax
import jax.numpy as jnp
from jax import lax
from jax.sharding import PartitionSpec as P


def on_device(
    features,
    bases,
    root,
    coeffs,
    tiles,
    tile_dst,
    tile_src,
    tile_rel,
    tile_live,
    send_list,
    cotangent,
):
    highest = lax.Precision.HIGHEST
    contract_first = (((0,), (0,)), ((), ()))
    feat_width = features.shape[1]
    size_block = tiles.shape[-1]
    blocks = features.reshape(-1, size_block, feat_width)
    local_blocks = blocks.shape[0]
    num_bases = bases.shape[0]
    slots_peer = send_list.shape[-1]
    row_devices = lax.axis_size("rows")
    total_slots = row_devices * slots_peer
    count_tiles = tiles.shape[2]
    adjacency = tiles[0, 0]
    dst_ids = tile_dst[0, 0]
    src_ids = tile_src[0, 0]
    rel_ids = tile_rel[0, 0]
    live_count = tile_live[0, 0]
    send_rows = send_list[0, 0]
    outgoing = blocks[send_rows]
    incoming = lax.all_to_all(outgoing, "rows", split_axis=0, concat_axis=0, tiled=True)
    received = incoming.reshape(total_slots, size_block, feat_width)
    step_tiles = math.gcd(count_tiles, 64)
    steps_live = (live_count + step_tiles - 1) // step_tiles

    def tile_weights(first_tile):
        position = first_tile + jnp.arange(step_tiles)
        in_use = (position < live_count).astype(jnp.float32)
        rel_hot = (rel_ids[:, None] == jnp.arange(coeffs.shape[0])[None, :]).astype(jnp.float32)
        coef_rows = jnp.dot(rel_hot, coeffs, precision=highest)
        dst_hot = (dst_ids[:, None] == jnp.arange(local_blocks)[None, :]).astype(
            jnp.float32
        ) * in_use[:, None]
        return (dst_hot[:, :, None] * coef_rows[:, None, :]).reshape(
            step_tiles, local_blocks * num_bases
        )

    def forward_step(block_index, running):
        first_tile = block_index * step_tiles
        sources = received[src_ids]
        messages = jnp.einsum(
            "tij,tjf->tif", adjacency, sources, preferred_element_type=jnp.float32
        )
        weights = tile_weights(first_tile)
        return running + lax.dot_general(
            weights, messages.reshape(step_tiles, -1), contract_first, precision=highest
        )

    zero_total = jnp.zeros((local_blocks * num_bases, size_block * feat_width), jnp.float32)
    partial_value = lax.fori_loop(0, steps_live, forward_step, zero_total)
    partial_value = partial_value.reshape(local_blocks, num_bases, size_block, feat_width)
    basis_f32 = bases.astype(jnp.float32)
    cot_blocks = cotangent.reshape(local_blocks, size_block, feat_width)
    cot_f32 = cot_blocks.astype(jnp.float32)
    root_term = jnp.dot(features, root, preferred_element_type=jnp.float32)
    rel_devices = lax.axis_size("rel")
    part_rows = features.shape[0] // rel_devices
    first_row = lax.axis_index("rel") * part_rows
    feat_part = lax.dynamic_slice_in_dim(features, first_row, part_rows)
    cot_part = lax.dynamic_slice_in_dim(cotangent, first_row, part_rows)
    root_local = lax.dot_general(
        feat_part, cot_part, contract_first, preferred_element_type=jnp.float32
    )
    projected_part = jnp.einsum("lbnf,bfg->lng", partial_value, basis_f32, precision=highest)
    basis_local = jnp.einsum("lbnf,lng->bfg", partial_value, cot_f32, precision=highest)
    projected = lax.psum(projected_part, "rel")
    basis_grad, root_grad = lax.psum((basis_local, root_local), ("rows", "rel"))
    output = (projected.reshape(-1, feat_width) + root_term).astype(jnp.bfloat16)
    agg_grad = jnp.einsum("lng,bfg->lbnf", cot_blocks, bases, preferred_element_type=jnp.float32)
    agg_grad = agg_grad.reshape(local_blocks * num_bases, size_block * feat_width)

    def backward_step(block_index, running):
        first_tile = block_index * step_tiles
        weights = tile_weights(first_tile)
        spread = jnp.dot(weights, agg_grad, precision=highest).astype(jnp.bfloat16)
        spread = spread.reshape(step_tiles, size_block, feat_width)
        backward_term = jnp.einsum(
            "tij,tif->tjf", adjacency, spread, preferred_element_type=jnp.float32
        )
        slot_hot = (src_ids[:, None] == jnp.arange(total_slots)[None, :]).astype(jnp.float32)
        return running + lax.dot_general(
            slot_hot, backward_term.reshape(step_tiles, -1), contract_first, precision=highest
        )

    slot_zero = jnp.zeros((total_slots, size_block * feat_width), jnp.float32)
    slot_grads = lax.fori_loop(0, steps_live, backward_step, slot_zero)
    returned = lax.all_to_all(
        slot_grads.reshape(row_devices, slots_peer, size_block * feat_width),
        "rows",
        split_axis=0,
        concat_axis=0,
        tiled=True,
    )
    block_hot = (send_rows.reshape(-1)[None, :] == jnp.arange(local_blocks)[:, None]).astype(
        jnp.float32
    )
    own_grads = jnp.dot(block_hot, returned.reshape(total_slots, -1), precision=highest)
    own_grads, projected = lax.optimization_barrier((own_grads, projected))
    summed = lax.psum(own_grads, "rel")
    root_back = lax.dot_general(
        cotangent, root, (((1,), (1,)), ((), ())), preferred_element_type=jnp.float32
    )
    feature_grad = summed.reshape(-1, feat_width) + root_back
    return (output, feature_grad, basis_grad, root_grad)


def solution(mesh):
    return jax.shard_map(
        on_device,
        mesh=mesh,
        in_specs=(
            P("rows", None),
            P(),
            P(),
            P("rel", None),
            P("rows", "rel", None, None, None),
            P("rows", "rel", None),
            P("rows", "rel", None),
            P("rows", "rel", None),
            P("rows", "rel"),
            P("rows", "rel", None, None),
            P("rows", None),
        ),
        out_specs=(P("rows", None), P("rows", None), P(), P()),
        check_vma=False,
    )
```

profile of v0, /device:TPU:1, one launch (start us, length us, event | category | flops | bytes accessed | tf_op | source)
XLA Modules:
  0.0 444.5 jit_solution(7627320191184519020)
XLA Ops:
  7.2 0.0 copy-start
  7.2 0.8 compare_select_fusion
  8.0 0.1 copy.24
  8.0 0.1 reshape.248
  8.2 3.7 gather_fusion
  11.9 9.6 %all-to-all-start = ((bf16[32,2,128,256]{3,2,1,0:T(8,128)(2,1)}), bf16[32,2,128,256]{3,2,1,0:T(8,128)(2,1)}, u32[]{:S(2)}, u32[]{:S(2)}) async-start(bf16[32,2,128,256]{3,2,1,0:T(8,128)(2,1)} %bitcast.121), calls=%async_computation | async-start | bytes 8388608 | tf_op jit(solution)/shard_map/all_to_all | solution.py:39
  22.1 0.0 copy-done
  22.2 0.0 copy-done.4
  22.2 2.7 convolution_bitcast_fusion.1
  24.8 5.5 %copy.36 = f32[4,8,128,256]{3,1,2,0:T(8,128)} copy(f32[4,8,128,256]{2,3,0,1:T(8,128)} %convolution_bitcast_fusion.1) | data formatting | bytes 8388608
  30.4 0.0 copy-done.12
  30.4 0.0 copy-done.13
  30.4 0.2 fusion.27
  30.6 4.0 broadcast_in_dim.5
  34.5 0.0 copy-done.9
  34.5 0.0 copy-done.10
  34.5 40.2 %while.25 = (s32[]{:T(128)}, f32[64,32768]{1,0:T(8,128)}, s32[]{:T(128)}, s32[1,1,64]{2,1,0:T(1,128)S(1)}, s32[1,1,64]{2,1,0:T(1,128)S(1)}, /*index=5*/s32[]{:T(...) while((s32[]{:T(128)}, f32[64,32768]{1,0:T(8,128)}, ...), condition=%wide.region_4.5_spmd, body=%wide.region_3.4_spmd.sunk | while | flops 2956991232 | bytes 73405568 | solution.py:104
  35.0 0.7 compare_convert_fusion.5
  35.7 8.6 %convolution_convert_fusion.2 = bf16[64,32768]{1,0:T(8,128)(2,1)S(1)} fusion(f32[32,32768]{1,0:T(8,128)} %get-tuple-element.440, f32[64,8]{0,1:T(8,128)S(1)} %get-tuple-element.439, f32[64,4]{0,1:T(4,128)S(1)} %fusion.72), kind=kOutput, calls=%fused_computation.11.clone.1 | convolution fusion | flops 807405568 | bytes 8391680 | tf_op jit(solution)/shard_map/while/body/dot_general | solution.py:93
  44.2 1.1 copy.51
  45.3 6.1 %convolution_bitcast_fusion.3 = f32[64,128,256]{1,2,0:T(8,128)} fusion(bf16[64,128,256]{2,1,0:T(8,128)(2,1)S(1)} %bitcast.115, bf16[64,128,128]{2,1,0:T(8,128)(2,1)} %get-tuple-element.441), kind=kOutput, calls=%fused_computation.12.clone.1 | convolution fusion | flops 536870912 | bytes 14680064 | tf_op jit(solution)/shard_map/while/body/tij,tif->tjf/dot_general | solution.py:95
  51.5 9.2 %copy.52 = f32[8,8,128,256]{3,1,2,0:T(8,128)} copy(f32[8,8,128,256]{2,3,1,0:T(8,128)} %bitcast.113) | data formatting | bytes 16777216 | tf_op jit(solution)/shard_map/while
  60.7 14.1 %convolution_add_fusion.7 = f32[64,32768]{1,0:T(8,128)} fusion(f32[64,32768]{1,0:T(8,128)} %get-tuple-element.423, f32[64,32768]{1,0:T(8,128)} %bitcast.112, s32[64]{0:T(128)S(1)} %bitcast.127), kind=kOutput, calls=%fused_computation.10.clone.1 | convolution fusion | flops 1612713984 | bytes 25166080 | tf_op jit(solution)/shard_map/while/body/dot_general | solution.py:99
  74.8 10.6 %reshape.243 = f32[32,2,32768]{2,1,0:T(2,128)} reshape(f32[64,32768]{1,0:T(8,128)} %get-tuple-element.237) | data formatting | bytes 16777216 | tf_op jit(solution)/shard_map/reshape | solution.py:106
  85.4 0.0 all-to-all-done
  85.4 7.4 %all-to-all-start.1 = ((f32[32,2,32768]{2,1,0:T(2,128)}), f32[32,2,32768]{2,1,0:T(2,128)}, u32[]{:S(2)}, u32[]{:S(2)}) async-start(f32[32,2,32768]{2,1,0:T(2,128)} %reshape.243), calls=%async_computation.1 | async-start | bytes 16777216 | tf_op jit(solution)/shard_map/all_to_all | solution.py:105
  92.9 0.0 all-reduce.5.cloned.1.call-start
  92.9 4.9 %gather_fusion.1 = bf16[64,128,256]{2,1,0:T(8,128)(2,1)} fusion(bf16[64,128,256]{2,1,0:T(8,128)(2,1)} %bitcast.12, s32[1024]{0:T(1024)S(1)} %pad_clamp_fusion), kind=kCustom, calls=%fused_computation.1 | custom fusion | bytes 8388864 | tf_op jit(solution)/shard_map/while/body/gather | solution.py:58
  97.9 2.3 broadcast_in_dim.4
  100.1 18.3 %while.24 = (s32[]{:T(128)}, f32[32,32768]{1,0:T(8,128)}, s32[]{:T(128)}, s32[1,1,64]{2,1,0:T(1,128)S(1)}, s32[]{:T(128)}, /*index=5*/f32[64,8]{0,1:T(8,128)S(1)...) while((s32[]{:T(128)}, f32[32,32768]{1,0:T(8,128)}, s32[]{:T(128)}, ...), condition=%wide.region_1.2_spmd, body=%wide.region_0.1_spmd.sunk | while | flops 1343228672 | bytes 81793968 | solution.py:68
  100.1 0.6 compare_convert_fusion.4
  100.8 4.1 fusion.65
  104.9 0.0 copy-start.1
  104.9 4.7 %copy.50 = f32[8,8,128,256]{3,1,2,0:T(8,128)S(1)} copy(f32[8,8,128,256]{3,2,1,0:T(8,128)S(1)} %bitcast.114) | data formatting | bytes 16777216 | tf_op jit(solution)/shard_map/while
  109.6 0.0 copy-done.1
  109.6 6.6 %convolution_add_fusion.6 = f32[32,32768]{1,0:T(8,128)S(1)} fusion(f32[32,32768]{1,0:T(8,128)S(1)} %copy-done.1, f32[64,32768]{1,0:T(8,128)S(1)} %bitcast.111, f32[64,8]{0,1:T(8,128)S(1)} %get-tuple-element.406, f32[64,4]{0,1:T(4,128)S(1)} %fusion.66), kind=kOutput, calls=%fused_computation.2.clone.1 | convolution fusion | flops 806356992 | bytes 16780288 | tf_op jit(solution)/shard_map/while/body/dot_general | solution.py:63
  116.3 0.0 copy-start.2
  116.3 2.0 copy-done.2
  118.4 0.0 copy-start.11
  118.4 6.0 %fusion.18 = f32[4,128,256]{2,1,0:T(8,128)} fusion(f32[4,8,128,256]{3,1,2,0:T(8,128)} %bitcast.117, bf16[8,256,256]{2,1,0:T(8,128)(2,1)S(1)} %copy-done), kind=kOutput, calls=%fused_computation.28 | convolution fusion | flops 3221225472 | bytes 5767168 | tf_op jit(solution)/shard_map/lbnf,bfg->lng/dot_general | solution.py:82
  124.4 0.0 all-reduce.5.cloned.1.call-update
  124.4 0.0 all-reduce.7.cloned.1.call-start
  124.5 0.1 copy.26
  124.6 0.1 eq.116
  124.7 75.4 %all-to-all-done.1 = f32[32,2,32768]{2,1,0:T(2,128)} async-done(((f32[32,2,32768]{2,1,0:T(2,128)}), f32[32,2,32768]{2,1,0:T(2,128)}, u32[]{:S(2)}, u32[]{:S(2)}) %all-to-all-start.1) | async-done | bytes 8388640 | tf_op jit(solution)/shard_map/all_to_all | solution.py:105
  200.1 10.9 %reshape.244 = f32[64,32768]{1,0:T(8,128)} reshape(f32[32,2,32768]{2,1,0:T(2,128)} %all-to-all-done.1) | data formatting | bytes 16777216 | tf_op jit(solution)/shard_map/reshape | solution.py:115
  211.0 6.2 %fusion.29 = f32[4,32768]{1,0:T(4,128)S(1)} fusion(f32[64,32768]{1,0:T(8,128)} %reshape.244, s32[64]{0:T(128)S(1)} %eq.116), kind=kOutput, calls=%fused_computation.45 | convolution fusion | flops 100663552 | bytes 8913152 | tf_op jit(solution)/shard_map/dot_general | solution.py:115
  217.2 0.0 all-reduce.5.cloned.1.call-done
  217.2 1.2 reshape.245
  218.4 0.0 all-reduce.7.cloned.1.call-update
  218.4 0.3 all-reduce.9.cloned.1.call-start
  218.7 0.0 copy-done.3
  218.7 0.0 copy-done.5
  218.7 0.9 fusion.24
  219.6 7.6 %fusion.15 = f32[8,256,256]{2,1,0:T(8,128)} fusion(bf16[4,128,256,1]{2,1,0,3:T(8,128)(2,1)S(1)} %bitcast.123, f32[4,8,128,256]{3,1,2,0:T(8,128)} %bitcast.118), kind=kOutput, calls=%fused_computation.27 | convolution fusion | flops 3221225472 | bytes 6553600 | tf_op jit(solution)/shard_map/lbnf,lng->bfg/dot_general | solution.py:83
  227.3 0.0 all-reduce.9.cloned.1.call-update
  227.3 0.0 copy-done.6
  227.3 0.0 copy-done.7
  227.3 0.9 fusion.21
  228.2 45.5 %all-reduce.7.cloned.1.call-done = f32[512,256]{1,0:T(8,128)} async-done(((f32[512,256]{1,0:T(8,128)}), f32[512,256]{1,0:T(8,128)}) %all-reduce.7.cloned.1.call-update) | async-done | bytes 524304 | tf_op jit(solution)/shard_map/psum | solution.py:117
  273.7 2.1 convolution_add_fusion.2
  275.8 158.1 %all-reduce.9.cloned.1.call-done = (f32[8,256,256]{2,1,0:T(8,128)}, f32[256,256]{1,0:T(8,128)}) async-done(((f32[8,256,256]{2,1,0:T(8,128)}, f32[256,256]{1,0:T(8,128)}), (f32[8,256,256]{2,1,0:T(8,128)}, f32[256,256]{1,0:T(8,128)})) %all-reduce.9.cloned.1.call-update) | async-done | bytes 2359312 | tf_op jit(solution)/shard_map/psum | solution.py:85
  433.9 3.1 copy.70
  437.0 0.7 copy.71
  (17 shorter events, 0.0 us)
Async XLA Ops:
  7.2 15.0 %copy-start = (bf16[8,256,256]{2,1,0:T(8,128)(2,1)S(1)}, bf16[8,256,256]{2,1,0:T(8,128)(2,1)}, u32[]{:S(2)}) copy-start(bf16[8,256,256]{2,1,0:T(8,128)(2,1)} %param.16) | copy-start | bytes 3145732
  11.9 10.3 %copy-start.4 = (bf16[512,256]{1,0:T(8,128)(2,1)S(1)}, bf16[512,256]{1,0:T(8,128)(2,1)}, u32[]{:S(2)}) copy-start(bf16[512,256]{1,0:T(8,128)(2,1)} %param.25) | copy-start | bytes 786436
  11.9 73.5 %all-to-all-start = ((bf16[32,2,128,256]{3,2,1,0:T(8,128)(2,1)}), bf16[32,2,128,256]{3,2,1,0:T(8,128)(2,1)}, u32[]{:S(2)}, u32[]{:S(2)}) async-start(bf16[32,2,128,256]{3,2,1,0:T(8,128)(2,1)} %bitcast.121), calls=%async_computation | async-start | bytes 8388608 | tf_op jit(solution)/shard_map/all_to_all | solution.py:39
  24.8 5.5 %copy-start.12 = (f32[200,8]{0,1:T(8,128)S(1)}, f32[200,8]{0,1:T(8,128)}, u32[]{:S(2)}) copy-start(f32[200,8]{0,1:T(8,128)} %param.18) | copy-start | bytes 19204
  24.8 5.5 %copy-start.13 = (s32[1,1,64]{2,1,0:T(1,128)S(1)}, s32[1,1,64]{2,1,0:T(1,128)}, u32[]{:S(2)}) copy-start(s32[1,1,64]{2,1,0:T(1,128)} %param.22) | copy-start | bytes 772
  30.6 4.0 copy-start.9
  30.6 4.0 copy-start.10
  85.4 114.7 %all-to-all-start.1 = ((f32[32,2,32768]{2,1,0:T(2,128)}), f32[32,2,32768]{2,1,0:T(2,128)}, u32[]{:S(2)}, u32[]{:S(2)}) async-start(f32[32,2,32768]{2,1,0:T(2,128)} %reshape.243), calls=%async_computation.1 | async-start | bytes 16777216 | tf_op jit(solution)/shard_map/all_to_all | solution.py:105
  92.9 124.4 %all-reduce.5.cloned.1.call-start = ((), (), s32[]{:S(2)}) async-start(), calls=%async_computation.2 | async-start | bytes 1048576 | tf_op jit(solution)/shard_map/psum | solution.py:84
  104.9 4.8 %copy-start.1 = (f32[32,32768]{1,0:T(8,128)S(1)}, f32[32,32768]{1,0:T(8,128)}, u32[]{:S(2)}) copy-start(f32[32,32768]{1,0:T(8,128)} %get-tuple-element.392) | copy-start | bytes 12582916 | tf_op jit(solution)/shard_map/while
  116.3 2.0 copy-start.2
  118.4 6.1 %copy-start.11 = (s32[1,1,32,2]{2,3,1,0:T(2,128)S(1)}, s32[1,1,32,2]{2,3,1,0:T(2,128)}, u32[]{:S(2)}) copy-start(s32[1,1,32,2]{2,3,1,0:T(2,128)} %param.24) | copy-start | bytes 772
  124.4 149.3 %all-reduce.7.cloned.1.call-start = ((), (), s32[]{:S(2)}) async-start(), calls=%async_computation.3 | async-start | bytes 1048576 | tf_op jit(solution)/shard_map/psum | solution.py:117
  211.0 7.7 %copy-start.3 = (bf16[512,256]{1,0:T(8,128)(2,1)S(1)}, bf16[512,256]{1,0:T(8,128)(2,1)}, u32[]{:S(2)}) copy-start(bf16[512,256]{1,0:T(8,128)(2,1)} %param.15) | copy-start | bytes 786436
  211.0 7.7 %copy-start.5 = (bf16[512,256]{1,0:T(8,128)(2,1)S(1)}, bf16[512,256]{1,0:T(8,128)(2,1)}, u32[]{:S(2)}) copy-start(bf16[512,256]{1,0:T(8,128)(2,1)} %param.25) | copy-start | bytes 786436
  218.4 215.5 %all-reduce.9.cloned.1.call-start = ((), (), s32[]{:S(2)}) async-start(), calls=%async_computation.4 | async-start | bytes 4718592 | tf_op jit(solution)/shard_map/psum | solution.py:85
  219.6 7.7 %copy-start.6 = (f32[4,128,256]{2,1,0:T(8,128)S(1)}, f32[4,128,256]{2,1,0:T(8,128)}, u32[]{:S(2)}) copy-start(f32[4,128,256]{2,1,0:T(8,128)} %all-reduce.5.cloned.1.call-done) | copy-start | bytes 1572868
  219.6 7.7 %copy-start.7 = (bf16[256,256]{1,0:T(8,128)(2,1)S(1)}, bf16[256,256]{1,0:T(8,128)(2,1)}, u32[]{:S(2)}) copy-start(bf16[256,256]{1,0:T(8,128)(2,1)} %param.17) | copy-start | bytes 393220
  433.9 3.1 copy-start.8
Sparse Core Ops, SparseCore 0:
  124.6 42.8 all-reduce.4
  218.5 55.1 all-reduce.6
  279.2 154.6 all-reduce.8
where the time goes:
time: 448 us; the launch traced here: 444 us
  waiting for transfers between devices  279 us (62%)
  matrix products  66.1 us (15%)
  local copies, waits for them, and re-layouts  64.4 us (14%)
  starting transfers between devices  17.4 us (4%)
  between operations  14.8 us (3%)
    psum x1, waiting for transfers between devices, on_device(): basis_grad, root_grad = lax.psum((basis_local, root_local), ('rows', 'rel'))  158 us
    all_to_all x1, waiting for transfers between devices, on_device(): lax.all_to_all(slot_grads.reshape(row_devices, slots_peer, size_block * f...  75.4 us
    psum x1, waiting for transfers between devices, on_device(): summed = lax.psum(own_grads, 'rel')  45.5 us
    while x7, local copies, waits for them, and re-layouts  17 us
    dot_general x1, matrix products, backward_step(): lax.dot_general(slot_hot, backward_term.reshape(step_tiles, -1), contract...  14.1 us
    reshape x1, local copies, waits for them, and re-layouts, on_device(): returned.reshape(total_slots, -1)  10.9 us
    reshape x1, local copies, waits for them, and re-layouts, on_device(): slot_grads.reshape(row_devices, slots_peer, size_block * feat_width)  10.6 us
    all_to_all x1, starting transfers between devices, on_device(): lax.all_to_all(outgoing, 'rows', split_axis=0, concat_axis=0, tiled=True)  9.61 us
  transfers between devices with their start and end apart: 5, of which 3 were waited for; matrix products, arithmetic and copies ran while one was open for 27% of the time, Pallas kernels for 0%

commit v1 on v0

--- a/solution.py
+++ b/solution.py
@@ -114,7 +114,7 @@
     )
     own_grads = jnp.dot(block_hot, returned.reshape(total_slots, -1), precision=highest)
     own_grads, projected = lax.optimization_barrier((own_grads, projected))
-    summed = lax.psum(own_grads, "rel")
+    summed = jnp.sum(lax.all_gather(own_grads, "rel"), axis=0)
     root_back = lax.dot_general(
         cotangent, root, (((1,), (1,)), ((), ())), preferred_element_type=jnp.float32
     )

time: 448 us -> 414 us (0.924)
  waiting for transfers between devices: 279 us -> 243 us
    psum x1 -> x0, waiting for transfers between devices: 45.5 us -> none  [on_device(): summed = lax.psum(own_grads, 'rel')]
    all_gather x0 -> x1, waiting for transfers between devices: none -> 36.5 us  [on_device(): summed = jnp.sum(lax.all_gather(own_grads, 'rel'), axis=0)]
    psum x1, waiting for transfers between devices: 158 us -> 131 us  [on_device(): basis_grad, root_grad = lax.psum((basis_local, root_local), ('rows', 'rel'))]
  transfers between devices with their start and end apart: 5 -> 5, of which waited for: 3 -> 3; matrix products, arithmetic and copies ran while one was open for 27% -> 30% of each run, Pallas kernels for 0% -> 0%
where the time goes in v1:
time: 414 us; the launch traced here: 411 us
  waiting for transfers between devices  243 us (59%)
  matrix products  65.9 us (16%)
  local copies, waits for them, and re-layouts  63.6 us (15%)
  starting transfers between devices  17.4 us (4%)
  between operations  16.5 us (4%)
  other arithmetic  4.19 us (1%)
    psum x1, waiting for transfers between devices, on_device(): basis_grad, root_grad = lax.psum((basis_local, root_local), ('rows', 'rel'))  131 us
    all_to_all x1, waiting for transfers between devices, on_device(): lax.all_to_all(slot_grads.reshape(row_devices, slots_peer, size_block * f...  75.4 us
    all_gather x1, waiting for transfers between devices, on_device(): summed = jnp.sum(lax.all_gather(own_grads, 'rel'), axis=0)  36.5 us
    while x7, local copies, waits for them, and re-layouts  17 us
    dot_general x1, matrix products, backward_step(): lax.dot_general(slot_hot, backward_term.reshape(step_tiles, -1), contract...  14.1 us
    reshape x1, local copies, waits for them, and re-layouts, on_device(): returned.reshape(total_slots, -1)  10.9 us
    reshape x1, local copies, waits for them, and re-layouts, on_device(): slot_grads.reshape(row_devices, slots_peer, size_block * feat_width)  10.6 us
    all_to_all x1, starting transfers between devices, on_device(): lax.all_to_all(outgoing, 'rows', split_axis=0, concat_axis=0, tiled=True)  9.61 us
  transfers between devices with their start and end apart: 5, of which 3 were waited for; matrix products, arithmetic and copies ran while one was open for 30% of the time, Pallas kernels for 0%

profile of v1, /device:TPU:1, one launch (start us, length us, event | category | flops | bytes accessed | tf_op | source)
XLA Modules:
  0.0 410.8 jit_solution(710790758381918305)
XLA Ops:
  8.0 0.0 copy-start
  8.0 0.8 compare_select_fusion
  8.8 0.1 copy.31
  8.9 0.1 reshape.248
  9.0 3.7 gather_fusion
  12.7 9.6 %all-to-all-start = ((bf16[32,2,128,256]{3,2,1,0:T(8,128)(2,1)}), bf16[32,2,128,256]{3,2,1,0:T(8,128)(2,1)}, u32[]{:S(2)}, u32[]{:S(2)}) async-start(bf16[32,2,128,256]{3,2,1,0:T(8,128)(2,1)} %bitcast.122), calls=%async_computation | async-start | bytes 8388608 | tf_op jit(solution)/shard_map/all_to_all | solution.py:39
  23.0 0.0 copy-done
  23.0 0.0 copy-done.4
  23.0 2.7 convolution_bitcast_fusion.1
  25.7 5.5 %copy.43 = f32[4,8,128,256]{3,1,2,0:T(8,128)} copy(f32[4,8,128,256]{2,3,0,1:T(8,128)} %convolution_bitcast_fusion.1) | data formatting | bytes 8388608
  31.2 0.0 copy-done.12
  31.2 0.0 copy-done.13
  31.2 0.2 fusion.27
  31.4 4.0 broadcast_in_dim.5
  35.4 0.0 copy-done.9
  35.4 0.0 copy-done.10
  35.4 40.2 %while.25 = (s32[]{:T(128)}, f32[64,32768]{1,0:T(8,128)}, s32[]{:T(128)}, s32[1,1,64]{2,1,0:T(1,128)S(1)}, s32[1,1,64]{2,1,0:T(1,128)S(1)}, /*index=5*/s32[]{:T(...) while((s32[]{:T(128)}, f32[64,32768]{1,0:T(8,128)}, ...), condition=%wide.region_4.5_spmd, body=%wide.region_3.4_spmd.sunk | while | flops 2956991232 | bytes 73405568 | solution.py:104
  35.8 0.7 compare_convert_fusion.5
  36.5 8.6 %convolution_convert_fusion.2 = bf16[64,32768]{1,0:T(8,128)(2,1)S(1)} fusion(f32[32,32768]{1,0:T(8,128)} %get-tuple-element.440, f32[64,8]{0,1:T(8,128)S(1)} %get-tuple-element.439, f32[64,4]{0,1:T(4,128)S(1)} %fusion.72), kind=kOutput, calls=%fused_computation.11.clone.1 | convolution fusion | flops 807405568 | bytes 8391680 | tf_op jit(solution)/shard_map/while/body/dot_general | solution.py:93
  45.1 1.1 copy.58
  46.2 6.1 %convolution_bitcast_fusion.3 = f32[64,128,256]{1,2,0:T(8,128)} fusion(bf16[64,128,256]{2,1,0:T(8,128)(2,1)S(1)} %bitcast.116, bf16[64,128,128]{2,1,0:T(8,128)(2,1)} %get-tuple-element.441), kind=kOutput, calls=%fused_computation.12.clone.1 | convolution fusion | flops 536870912 | bytes 14680064 | tf_op jit(solution)/shard_map/while/body/tij,tif->tjf/dot_general | solution.py:95
  52.3 9.2 %copy.59 = f32[8,8,128,256]{3,1,2,0:T(8,128)} copy(f32[8,8,128,256]{2,3,1,0:T(8,128)} %bitcast.114) | data formatting | bytes 16777216 | tf_op jit(solution)/shard_map/while
  61.5 14.1 %convolution_add_fusion.7 = f32[64,32768]{1,0:T(8,128)} fusion(f32[64,32768]{1,0:T(8,128)} %get-tuple-element.423, f32[64,32768]{1,0:T(8,128)} %bitcast.113, s32[64]{0:T(128)S(1)} %bitcast.129), kind=kOutput, calls=%fused_computation.10.clone.1 | convolution fusion | flops 1612713984 | bytes 25166080 | tf_op jit(solution)/shard_map/while/body/dot_general | solution.py:99
  75.6 10.6 %reshape.243 = f32[32,2,32768]{2,1,0:T(2,128)} reshape(f32[64,32768]{1,0:T(8,128)} %get-tuple-element.237) | data formatting | bytes 16777216 | tf_op jit(solution)/shard_map/reshape | solution.py:106
  86.2 0.0 all-to-all-done
  86.2 7.4 %all-to-all-start.1 = ((f32[32,2,32768]{2,1,0:T(2,128)}), f32[32,2,32768]{2,1,0:T(2,128)}, u32[]{:S(2)}, u32[]{:S(2)}) async-start(f32[32,2,32768]{2,1,0:T(2,128)} %reshape.243), calls=%async_computation.1 | async-start | bytes 16777216 | tf_op jit(solution)/shard_map/all_to_all | solution.py:105
  93.7 0.0 all-reduce.4.cloned.1.call-start
  93.7 4.9 %gather_fusion.1 = bf16[64,128,256]{2,1,0:T(8,128)(2,1)} fusion(bf16[64,128,256]{2,1,0:T(8,128)(2,1)} %bitcast.12, s32[1024]{0:T(1024)S(1)} %pad_clamp_fusion), kind=kCustom, calls=%fused_computation.1 | custom fusion | bytes 8388864 | tf_op jit(solution)/shard_map/while/body/gather | solution.py:58
  98.7 2.3 broadcast_in_dim.4
  101.0 18.3 %while.24 = (s32[]{:T(128)}, f32[32,32768]{1,0:T(8,128)}, s32[]{:T(128)}, s32[1,1,64]{2,1,0:T(1,128)S(1)}, s32[]{:T(128)}, /*index=5*/f32[64,8]{0,1:T(8,128)S(1)...) while((s32[]{:T(128)}, f32[32,32768]{1,0:T(8,128)}, s32[]{:T(128)}, ...), condition=%wide.region_1.2_spmd, body=%wide.region_0.1_spmd.sunk | while | flops 1343228672 | bytes 81793968 | solution.py:68
  101.0 0.6 compare_convert_fusion.4
  101.6 4.1 fusion.65
  105.7 0.0 copy-start.1
  105.7 4.7 %copy.57 = f32[8,8,128,256]{3,1,2,0:T(8,128)S(1)} copy(f32[8,8,128,256]{3,2,1,0:T(8,128)S(1)} %bitcast.115) | data formatting | bytes 16777216 | tf_op jit(solution)/shard_map/while
  110.4 0.0 copy-done.1
  110.5 6.6 %convolution_add_fusion.6 = f32[32,32768]{1,0:T(8,128)S(1)} fusion(f32[32,32768]{1,0:T(8,128)S(1)} %copy-done.1, f32[64,32768]{1,0:T(8,128)S(1)} %bitcast.112, f32[64,8]{0,1:T(8,128)S(1)} %get-tuple-element.406, f32[64,4]{0,1:T(4,128)S(1)} %fusion.66), kind=kOutput, calls=%fused_computation.2.clone.1 | convolution fusion | flops 806356992 | bytes 16780288 | tf_op jit(solution)/shard_map/while/body/dot_general | solution.py:63
  117.1 0.0 copy-start.2
  117.1 2.0 copy-done.2
  119.2 0.0 copy-start.11
  119.3 6.0 %fusion.18 = f32[4,128,256]{2,1,0:T(8,128)} fusion(f32[4,8,128,256]{3,1,2,0:T(8,128)} %bitcast.118, bf16[8,256,256]{2,1,0:T(8,128)(2,1)S(1)} %copy-done), kind=kOutput, calls=%fused_computation.28 | convolution fusion | flops 3221225472 | bytes 5767168 | tf_op jit(solution)/shard_map/lbnf,bfg->lng/dot_general | solution.py:82
  125.2 0.0 all-reduce.4.cloned.1.call-update
  125.3 0.0 all-gather.4.cloned.1.call-start
  125.3 0.0 copy-done.11
  125.3 0.1 copy.33
  125.4 0.1 eq.116
  125.5 75.4 %all-to-all-done.1 = f32[32,2,32768]{2,1,0:T(2,128)} async-done(((f32[32,2,32768]{2,1,0:T(2,128)}), f32[32,2,32768]{2,1,0:T(2,128)}, u32[]{:S(2)}, u32[]{:S(2)}) %all-to-all-start.1) | async-done | bytes 8388640 | tf_op jit(solution)/shard_map/all_to_all | solution.py:105
  200.9 10.9 %reshape.244 = f32[64,32768]{1,0:T(8,128)} reshape(f32[32,2,32768]{2,1,0:T(2,128)} %all-to-all-done.1) | data formatting | bytes 16777216 | tf_op jit(solution)/shard_map/reshape | solution.py:115
  211.8 7.0 %fusion.29 = f32[4,32768]{1,0:T(4,128)} fusion(f32[64,32768]{1,0:T(8,128)} %reshape.244, s32[64]{0:T(128)S(1)} %eq.116), kind=kOutput, calls=%fused_computation.45 | convolution fusion | flops 100663552 | bytes 8913152 | tf_op jit(solution)/shard_map/dot_general | solution.py:115
  218.8 0.0 all-gather.4.cloned.1.call-update
  218.9 0.3 all-reduce.6.cloned.1.call-start
  219.1 0.0 copy-done.3
  219.1 0.0 copy-done.5
  219.2 0.9 fusion.24
  220.1 7.6 %fusion.15 = f32[8,256,256]{2,1,0:T(8,128)} fusion(bf16[4,128,256,1]{2,1,0,3:T(8,128)(2,1)S(1)} %bitcast.124, f32[4,8,128,256]{3,1,2,0:T(8,128)} %bitcast.119), kind=kOutput, calls=%fused_computation.27 | convolution fusion | flops 3221225472 | bytes 6553600 | tf_op jit(solution)/shard_map/lbnf,lng->bfg/dot_general | solution.py:83
  227.7 0.0 all-reduce.6.cloned.1.call-update
  227.7 0.9 fusion.21
  228.7 36.5 %all-gather.4.cloned.1.call-done = f32[4,4,32768]{2,1,0:T(4,128)} async-done(((f32[1,4,32768]{2,1,0:T(4,128)}), f32[4,4,32768]{2,1,0:T(4,128)}) %all-gather.4.cloned.1.call-update) | async-done | bytes 2097168 | tf_op jit(solution)/shard_map/all_gather | solution.py:117
  265.1 2.1 reduce_sum.9
  267.2 0.4 reshape.245
  267.6 1.1 convolution_add_fusion.2
  268.7 130.7 %all-reduce.6.cloned.1.call-done = (f32[8,256,256]{2,1,0:T(8,128)}, f32[256,256]{1,0:T(8,128)}) async-done(((f32[8,256,256]{2,1,0:T(8,128)}, f32[256,256]{1,0:T(8,128)}), (f32[8,256,256]{2,1,0:T(8,128)}, f32[256,256]{1,0:T(8,128)})) %all-reduce.6.cloned.1.call-update) | async-done | bytes 2359312 | tf_op jit(solution)/shard_map/psum | solution.py:85
  399.4 3.1 copy.76
  402.5 0.0 copy-done.8
  402.5 0.7 copy.77
  (18 shorter events, 0.0 us)
Async XLA Ops:
  8.0 15.0 %copy-start = (bf16[8,256,256]{2,1,0:T(8,128)(2,1)S(1)}, bf16[8,256,256]{2,1,0:T(8,128)(2,1)}, u32[]{:S(2)}) copy-start(bf16[8,256,256]{2,1,0:T(8,128)(2,1)} %param.16) | copy-start | bytes 3145732
  12.7 10.3 %copy-start.4 = (bf16[512,256]{1,0:T(8,128)(2,1)S(1)}, bf16[512,256]{1,0:T(8,128)(2,1)}, u32[]{:S(2)}) copy-start(bf16[512,256]{1,0:T(8,128)(2,1)} %param.25) | copy-start | bytes 786436
  12.7 73.5 %all-to-all-start = ((bf16[32,2,128,256]{3,2,1,0:T(8,128)(2,1)}), bf16[32,2,128,256]{3,2,1,0:T(8,128)(2,1)}, u32[]{:S(2)}, u32[]{:S(2)}) async-start(bf16[32,2,128,256]{3,2,1,0:T(8,128)(2,1)} %bitcast.122), calls=%async_computation | async-start | bytes 8388608 | tf_op jit(solution)/shard_map/all_to_all | solution.py:39
  25.7 5.5 %copy-start.12 = (f32[200,8]{0,1:T(8,128)S(1)}, f32[200,8]{0,1:T(8,128)}, u32[]{:S(2)}) copy-start(f32[200,8]{0,1:T(8,128)} %param.18) | copy-start | bytes 19204
  25.7 5.5 %copy-start.13 = (s32[1,1,64]{2,1,0:T(1,128)S(1)}, s32[1,1,64]{2,1,0:T(1,128)}, u32[]{:S(2)}) copy-start(s32[1,1,64]{2,1,0:T(1,128)} %param.22) | copy-start | bytes 772
  31.4 4.0 copy-start.9
  31.4 4.0 copy-start.10
  86.2 114.6 %all-to-all-start.1 = ((f32[32,2,32768]{2,1,0:T(2,128)}), f32[32,2,32768]{2,1,0:T(2,128)}, u32[]{:S(2)}, u32[]{:S(2)}) async-start(f32[32,2,32768]{2,1,0:T(2,128)} %reshape.243), calls=%async_computation.1 | async-start | bytes 16777216 | tf_op jit(solution)/shard_map/all_to_all | solution.py:105
  93.7 125.2 %all-reduce.4.cloned.1.call-start = ((), (), s32[]{:S(2)}) async-start(), calls=%async_computation.2 | async-start | bytes 1048576 | tf_op jit(solution)/shard_map/psum | solution.py:84
  105.7 4.8 %copy-start.1 = (f32[32,32768]{1,0:T(8,128)S(1)}, f32[32,32768]{1,0:T(8,128)}, u32[]{:S(2)}) copy-start(f32[32,32768]{1,0:T(8,128)} %get-tuple-element.392) | copy-start | bytes 12582916 | tf_op jit(solution)/shard_map/while
  117.1 2.0 copy-start.2
  119.2 6.1 %copy-start.11 = (s32[1,1,32,2]{2,3,1,0:T(2,128)S(1)}, s32[1,1,32,2]{2,3,1,0:T(2,128)}, u32[]{:S(2)}) copy-start(s32[1,1,32,2]{2,3,1,0:T(2,128)} %param.24) | copy-start | bytes 772
  125.3 139.9 %all-gather.4.cloned.1.call-start = ((), (), s32[]{:S(2)}) async-start(), calls=%async_computation.3 | async-start | bytes 2621440 | tf_op jit(solution)/shard_map/all_gather | solution.py:117
  211.8 7.3 %copy-start.3 = (bf16[512,256]{1,0:T(8,128)(2,1)S(1)}, bf16[512,256]{1,0:T(8,128)(2,1)}, u32[]{:S(2)}) copy-start(bf16[512,256]{1,0:T(8,128)(2,1)} %param.15) | copy-start | bytes 786436
  211.8 7.3 %copy-start.5 = (bf16[512,256]{1,0:T(8,128)(2,1)S(1)}, bf16[512,256]{1,0:T(8,128)(2,1)}, u32[]{:S(2)}) copy-start(bf16[512,256]{1,0:T(8,128)(2,1)} %param.25) | copy-start | bytes 786436
  218.9 180.5 %all-reduce.6.cloned.1.call-start = ((), (), s32[]{:S(2)}) async-start(), calls=%async_computation.4 | async-start | bytes 4718592 | tf_op jit(solution)/shard_map/psum | solution.py:85
  220.1 7.7 %copy-start.6 = (f32[4,128,256]{2,1,0:T(8,128)S(1)}, f32[4,128,256]{2,1,0:T(8,128)}, u32[]{:S(2)}) copy-start(f32[4,128,256]{2,1,0:T(8,128)} %all-reduce.4.cloned.1.call-done) | copy-start | bytes 1572868
  220.1 7.7 %copy-start.7 = (bf16[256,256]{1,0:T(8,128)(2,1)S(1)}, bf16[256,256]{1,0:T(8,128)(2,1)}, u32[]{:S(2)}) copy-start(bf16[256,256]{1,0:T(8,128)(2,1)} %param.17) | copy-start | bytes 393220
  399.4 3.1 copy-start.8
Sparse Core Ops, SparseCore 0:
  125.4 42.8 all-reduce.3
  219.0 46.1 all-gather.3
Sparse Core Ops, SparseCore 1:
  227.8 171.5 all-reduce.5
